TPU v7x, 32 devices: a whole 2x2x4 slice. The times are simulated.
32 devices in a mesh: space: 4 (over y, x), vel: 8 (over z, core).
Axes of the slice: x: 2, y: 2, z: 4, core: 2. Of those that a mesh axis runs over, the one named last changes fastest.
Arguments:
- distribution: float32 [256, 64, 4096], P('space', None, 'vel'), may hold values from -6 to 6
- inverse_jacobian: float32 [256, 3, 3], P('space'), may hold values from -1 to 1
- density: float32 [256, 64], P('space'), may hold values from 1 to 10
- collision_blocks: float32 [32, 6, 128, 128], replicated, may hold values from -0.21875 to 0.21875
- block_columns: int32 [32, 6], replicated, may hold values from 0 to 31, as said below
- send_lists: int32 [4, 4, 48], P('space'), may hold values from 0 to 383, as said below
- exterior_faces: int32 [256, 6], P('space'), may hold values from 0 to 576, as said below
Outputs:
- advanced: float32 [256, 64, 4096], P('space', None, 'vel')
Inputs may be any that keep to these rules, and one draw needn't show every extreme that they name: `block_columns`: each row b lists 6 different block columns, the first being b itself. send_lists[q, p] holds different faces (6 e + s, e local to q) in its first slots and 0 in the slots after them; send_lists[p, p] is all 0. Every used slot is read by exactly one face of partition p, and slots after the used ones are read by none. `exterior_faces`: an entry below 384 names a face 6 e + s of the partition's own elements; 384 + q * 48 + j names slot j of the list partition q sends to this partition; 576 marks a wall, whose exterior trace is zero. Exactly 32 faces of each partition are walls.
All inputs are finite; a program needn't handle non-finite values.
Results may differ from a plain program's by a relative error of at most 0.0003.
Values sent between devices are 32-bit elements; how exact they have to be, the bound alone decides.
No kernel may reach another device: no remote copies, remote signals or barrier semaphores. Data moves between devices by JAX's collectives and lax.ppermute only.
A program may use at most 256 MiB of HBM per device.

v0:
```python
import jax
import jax.numpy as jnp
import numpy as np
from jax import lax
from jax.sharding import PartitionSpec as P

VG = 16
TIME_STEP = 0.03
LIFT_SCALE = 6.0


def lagrange_derivative():
    points = np.array([-1.0, -1.0 / np.sqrt(5.0), 1.0 / np.sqrt(5.0), 1.0])
    barycentric = np.ones(4)
    for column in range(4):
        for second in range(4):
            if second != column:
                barycentric[column] = barycentric[column] / (points[column] - points[second])
    matrix = np.zeros((4, 4))
    for row_node in range(4):
        for col_node in range(4):
            if row_node != col_node:
                matrix[row_node, col_node] = (
                    barycentric[col_node]
                    / barycentric[row_node]
                    / (points[row_node] - points[col_node])
                )
        matrix[row_node, row_node] = -np.sum(matrix[row_node])
    return matrix


def derivative_stack():
    single = lagrange_derivative()
    identity = np.eye(4)
    stacked = np.concatenate(
        [
            np.kron(np.kron(single, identity), identity),
            np.kron(np.kron(identity, single), identity),
            np.kron(np.kron(identity, identity), single),
        ],
        0,
    )
    return jnp.asarray(stacked, dtype=jnp.float32)


def grid_velocities(first_id, amount):
    velocity_id = first_id + jnp.arange(amount, dtype=jnp.int32)
    components = [velocity_id // (VG * VG), velocity_id // VG % VG, velocity_id % VG]
    return [
        3.0 * ((2.0 * component.astype(jnp.float32) + 1.0) / VG - 1.0) for component in components
    ]


def face_speeds(inverse_jacobian, velocity_x, velocity_y, velocity_z):
    return (
        inverse_jacobian[:, :, 0, None] * velocity_x[None, None, :]
        + inverse_jacobian[:, :, 1, None] * velocity_y[None, None, :]
        + inverse_jacobian[:, :, 2, None] * velocity_z[None, None, :]
    )


def face_values(node_field):
    node_cube = node_field.reshape(node_field.shape[0], 4, 4, 4, node_field.shape[2])
    face_list = [
        node_cube[:, 0],
        node_cube[:, 3],
        node_cube[:, :, 0],
        node_cube[:, :, 3],
        node_cube[:, :, :, 0],
        node_cube[:, :, :, 3],
    ]
    return jnp.stack(face_list, 1).reshape(node_field.shape[0], 6, 16, node_field.shape[2])


def lift_faces(face_flux):
    elements = face_flux.shape[0]
    columns = face_flux.shape[3]
    blocks = face_flux.reshape(elements, 6, 4, 4, columns)
    summed = jnp.zeros((elements, 4, 4, 4, columns), jnp.float32)
    for face_id in range(6):
        direction = face_id // 2
        placed = jnp.expand_dims(blocks[:, face_id], 1 + direction)
        padding = [(0, 0), (0, 0), (0, 0), (0, 0), (0, 0)]
        padding[1 + direction] = (0, 3) if face_id % 2 == 0 else (3, 0)
        summed = summed + jnp.pad(placed, padding)
    return summed.reshape(elements, 64, columns)


def advection(node_field, speeds, interior, outside):
    stacked = derivative_stack()
    derived = jnp.einsum("mn,env->emv", stacked, node_field, precision=lax.Precision.HIGHEST)
    derived = derived.reshape(node_field.shape[0], 3, node_field.shape[1], node_field.shape[2])
    volume = -(
        speeds[:, 0, None, :] * derived[:, 0]
        + speeds[:, 1, None, :] * derived[:, 1]
        + speeds[:, 2, None, :] * derived[:, 2]
    )
    face_signs = jnp.asarray(np.array([-1.0, 1.0, -1.0, 1.0, -1.0, 1.0]), dtype=jnp.float32)
    normal = jnp.repeat(speeds, 2, axis=1) * face_signs[None, :, None]
    weight = LIFT_SCALE * jnp.minimum(normal, 0.0)
    face_flux = weight[:, :, None, :] * (interior - outside)
    return volume + lift_faces(face_flux)


def collide(node_block, collision_blocks, block_columns):
    block_rows = collision_blocks.shape[0]
    block_count = collision_blocks.shape[1]
    width = collision_blocks.shape[2]
    flat_rows = node_block.reshape(-1, node_block.shape[-1])
    outputs = []
    for block_id in range(block_rows):
        total = jnp.zeros((flat_rows.shape[0], width), jnp.float32)
        for slot in range(block_count):
            start = block_columns[block_id, slot] * width
            piece = lax.dynamic_slice_in_dim(flat_rows, start, width, 1)
            total = total + lax.dot_general(
                piece,
                collision_blocks[block_id, slot],
                (((1,), (1,)), ((), ())),
                precision=lax.Precision.HIGHEST,
                preferred_element_type=jnp.float32,
            )
        outputs.append(total)
    applied = jnp.concatenate(outputs, 1).reshape(node_block.shape)
    return applied - node_block


def body(
    distribution,
    inverse_jacobian,
    density,
    collision_blocks,
    block_columns,
    send_lists,
    exterior_faces,
):
    vel_id = lax.axis_index("vel")
    span_local = distribution.shape[2]
    velocity = grid_velocities(vel_id * span_local, span_local)
    speeds = face_speeds(inverse_jacobian, velocity[0], velocity[1], velocity[2])
    send_rows = send_lists[0]
    lookup = exterior_faces.reshape(-1)

    def advect(node_field):
        interior = face_values(node_field)
        table_own = interior.reshape(-1, 16, span_local)
        outgoing = jnp.take(table_own, send_rows, axis=0)
        incoming = lax.all_to_all(outgoing, "space", split_axis=0, concat_axis=0, tiled=True)
        face_table = jnp.concatenate(
            [
                table_own,
                incoming.reshape(-1, 16, span_local),
                jnp.zeros((1, 16, span_local), jnp.float32),
            ],
            0,
        )
        outside = jnp.take(face_table, lookup, axis=0).reshape(interior.shape)
        return advection(node_field, speeds, interior, outside)

    def on_nodes(node_block):
        change = collide(node_block, collision_blocks, block_columns)
        returned = lax.all_to_all(change, "vel", split_axis=2, concat_axis=1, tiled=True)
        return (returned, node_block, change)

    def to_nodes(node_field):
        return on_nodes(lax.all_to_all(node_field, "vel", split_axis=1, concat_axis=2, tiled=True))

    scaling = density[:, :, None]
    flow_zero = advect(distribution)
    back_zero, nodes_zero, change_zero = to_nodes(distribution)
    first_section = distribution + TIME_STEP * (flow_zero + scaling * back_zero)
    flow_one = advect(first_section)
    back_one = to_nodes(first_section)[0]
    return 0.5 * distribution + 0.5 * (first_section + TIME_STEP * (flow_one + scaling * back_one))


def solution(mesh):
    in_specs = (
        P("space", None, "vel"),
        P("space", None, None),
        P("space", None),
        P(),
        P(),
        P("space", None, None),
        P("space", None),
    )
    out_specs = P("space", None, "vel")
    return jax.shard_map(body, mesh=mesh, in_specs=in_specs, out_specs=out_specs, check_vma=False)
```

profile of v0, /device:TPU:0, one launch (start us, length us, event | category | flops | bytes accessed | tf_op | source)
XLA Modules:
  0.0 1381.4 jit_solution(17776754912822584726)
XLA Ops:
  0.0 11.6 copy.231
  156.2 15.2 %copy.198 = f32[64,6,4,4,512]{4,3,2,1,0:T(4,128)} copy(f32[64,6,4,4,512]{4,0,3,2,1:T(8,128)S(1)} %fusion.37) | data formatting | bytes 25165824 | tf_op jit(solution)/shard_map/stack | solution.py:72
  171.4 14.7 %reshape_reshape.6 = f32[384,16,512]{2,1,0:T(8,128)} reshape(f32[64,6,4,4,512]{4,3,2,1,0:T(4,128)} %copy.198) | data formatting | bytes 25165824 | tf_op jit(solution)/shard_map/reshape;reshape | solution.py:146
  186.3 8.2 gather_fusion
  208.1 8.4 copy.207
  335.5 8.9 copy.208
  344.4 11.3 bitcast_subtract_fusion.1
  355.7 13.3 copy.209
  369.0 15.4 %reshape.653 = f32[8,1,262144]{2,1,0:T(1,128)} reshape(f32[4096,8,64]{2,1,0:T(8,128)} %bitcast.1762) | data formatting | bytes 16777216
  390.8 25.1 %fusion.1745 = f32[192,64,512]{2,0,1:T(8,128)} fusion(f32[192,64,1]{0,1,2:T(8,128)S(1)} %copy-done.21, f32[64,64,512]{2,1,0:T(8,128)} %param.15), kind=kOutput, calls=%fused_computation.2140 | convolution fusion | flops 4831838208 | bytes 33603584 | tf_op jit(solution)/shard_map/mn,env->emv/dot_general | solution.py:91
  416.0 18.2 %fusion.1731 = (f32[64,1,64,512]{3,2,1,0:T(8,128)}, f32[64,1,64,512]{3,2,1,0:T(8,128)}, f32[64,1,64,512]{3,2,1,0:T(8,128)}) fusion(f32[64,3,64,512]{3,2,1,0:T(8,128)} %bitcast.1752), kind=kLoop, calls=%fused_computation.2126 | loop fusion | bytes 50331648 | tf_op jit(solution)/shard_map/slice | solution.py:94
  434.2 16.1 %maximum_maximum_fusion = f32[577,16,512]{2,1,0:T(8,128)} fusion(f32[192,16,512]{2,1,0:T(8,128)} %bitcast.18, f32[384,16,512]{2,1,0:T(8,128)} %reshape_reshape.6, f32[577]{0:T(1024)S(1)} %pad.59.clone), kind=kLoop, calls=%fused_computation.4 | loop fusion | flops 9453568 | bytes 37783812 | tf_op jit(solution)/shard_map/concatenate | solution.py:149
  450.3 12.3 gather_fusion.1
  462.6 10.5 broadcast_select_fusion.1
  473.1 14.5 %reshape.590 = f32[64,6,4,4,512]{4,3,2,1,0:T(4,128)} reshape(f32[384,16,512]{2,1,0:T(8,128)} %broadcast_select_fusion.1) | data formatting | bytes 25165824 | tf_op jit(solution)/shard_map/reshape | solution.py:157
  487.5 13.9 %fusion.1 = f32[64,6,4,4,512]{4,0,3,2,1:T(8,128)S(1)} fusion(f32[64,6,4,4,512]{4,0,3,2,1:T(8,128)} %copy-done.5, f32[64,6,4,4,512]{4,3,2,1,0:T(4,128)} %reshape.590, f32[64,6,512]{2,0,1:T(8,128)S(1)} %fusion.106), kind=kLoop, calls=%fused_computation.9 | loop fusion | flops 6291456 | bytes 38535168 | tf_op jit(solution)/shard_map/mul | solution.py:101
  514.6 8.5 copy.204
  523.1 50.5 %all-to-all-done.2 = f32[8,1,262144]{2,1,0:T(1,128)} async-done(((f32[8,1,262144]{2,1,0:T(1,128)}), f32[8,1,262144]{2,1,0:T(1,128)}, u32[]{:S(2)}, u32[]{:S(2)}) %all-to-all-start.2) | async-done | bytes 8388640 | tf_op jit(solution)/shard_map/all_to_all | solution.py:162
  574.2 26.2 %reduce = f32[8,262144]{1,0:T(8,128)} reduce(f32[8,1,262144]{2,1,0:T(1,128)} %all-to-all-done.2, f32[]{:T(128)} %broadcast.344), dimensions={1}, to_apply=%all_to_all.63.reduce_sub_computation | reduce | bytes 16777220 | tf_op jit(solution)/shard_map/all_to_all | solution.py:162
  600.5 15.7 %reshape.654 = f32[4096,8,64]{2,1,0:T(8,128)} reshape(f32[8,262144]{1,0:T(8,128)} %reduce) | data formatting | bytes 16777216
  616.1 12.7 copy.210
  628.9 42.2 %fusion.27 = f32[64,64,512]{2,0,1:T(8,128)} fusion(f32[64,1,64,512]{3,2,1,0:T(8,128)} %get-tuple-element.12, f32[64,1,64,512]{3,2,1,0:T(8,128)} %get-tuple-element.11, f32[64,1,64,512]{3,2,1,0:T(8,128)} %get-tuple-element.10, f32[64,8,8,512]{3,0,1,2:T(8,128)} %copy.210, f32[64,4,4,4,512]{4,0,3,2,1:T(8,128)} %copy.204, f32[64,64]{0,1:T(8,128)S(1)} %copy.205, ...), kind=kLoop, calls=%fused_computation.43 | loop fusion | flops 23068672 | bytes 59129856 | tf_op jit(solution)/shard_map/add | solution.py:171
  686.2 15.2 %copy.220 = f32[64,6,4,4,512]{4,3,2,1,0:T(4,128)} copy(f32[64,6,4,4,512]{4,0,3,2,1:T(8,128)S(1)} %fusion.33) | data formatting | bytes 25165824 | tf_op jit(solution)/shard_map/stack | solution.py:72
  701.4 14.7 %reshape_reshape.7 = f32[384,16,512]{2,1,0:T(8,128)} reshape(f32[64,6,4,4,512]{4,3,2,1,0:T(4,128)} %copy.220) | data formatting | bytes 25165824 | tf_op jit(solution)/shard_map/reshape;reshape | solution.py:146
  716.1 8.2 gather_fusion.2
  730.3 129.6 %all-to-all-done.4 = f32[64,64,512]{2,0,1:T(8,128)} async-done(((f32[64,64,512]{2,0,1:T(8,128)}), f32[64,64,512]{2,0,1:T(8,128)}, u32[]{:S(2)}, u32[]{:S(2)}) %all-to-all-start.4) | async-done | bytes 8388640 | tf_op jit(solution)/shard_map/all_to_all | solution.py:166
  865.1 8.2 copy.353
  873.4 8.5 copy.256
  1005.1 9.5 all_to_all.71
  1041.3 9.0 copy.228
  1050.3 11.2 bitcast_subtract_fusion
  1061.6 13.3 copy.229
  1074.9 15.5 %reshape.655 = f32[8,1,262144]{2,1,0:T(1,128)} reshape(f32[4096,8,64]{2,1,0:T(8,128)} %bitcast.1764) | data formatting | bytes 16777216
  1095.5 29.9 %fusion.31 = f32[64,512,192]{1,2,0:T(8,128)} fusion(f32[192,64,1]{0,1,2:T(8,128)S(1)} %copy-done.22, f32[64,64,512]{2,0,1:T(8,128)} %fusion.27), kind=kOutput, calls=%fused_computation.55 | convolution fusion | flops 4831838208 | bytes 33603584 | tf_op jit(solution)/shard_map/mn,env->emv/dot_general | solution.py:91
  1125.4 18.3 %fusion.1730 = (f32[64,1,64,512]{3,2,1,0:T(8,128)}, f32[64,1,64,512]{3,2,1,0:T(8,128)}, f32[64,1,64,512]{3,2,1,0:T(8,128)}) fusion(f32[64,3,64,512]{3,2,1,0:T(8,128)} %bitcast.1753), kind=kLoop, calls=%fused_computation.2125 | loop fusion | bytes 50331648 | tf_op jit(solution)/shard_map/slice | solution.py:94
  1143.8 16.1 %maximum_maximum_fusion.1 = f32[577,16,512]{2,1,0:T(8,128)} fusion(f32[192,16,512]{2,1,0:T(8,128)} %bitcast.429, f32[384,16,512]{2,1,0:T(8,128)} %reshape_reshape.7, f32[577]{0:T(1024)S(1)} %copy-done.24), kind=kLoop, calls=%fused_computation.5 | loop fusion | flops 9453568 | bytes 37783812 | tf_op jit(solution)/shard_map/concatenate | solution.py:149
  1159.9 12.3 gather_fusion.3
  1172.2 10.5 broadcast_select_fusion
  1182.6 14.6 %reshape.597 = f32[64,6,4,4,512]{4,3,2,1,0:T(4,128)} reshape(f32[384,16,512]{2,1,0:T(8,128)} %broadcast_select_fusion) | data formatting | bytes 25165824 | tf_op jit(solution)/shard_map/reshape | solution.py:157
  1197.2 13.7 fusion
  1215.0 7.3 fusion.3
  1222.3 8.5 copy.226
  1230.8 48.6 %all-to-all-done.5 = f32[8,1,262144]{2,1,0:T(1,128)} async-done(((f32[8,1,262144]{2,1,0:T(1,128)}), f32[8,1,262144]{2,1,0:T(1,128)}, u32[]{:S(2)}, u32[]{:S(2)}) %all-to-all-start.5) | async-done | bytes 8388640 | tf_op jit(solution)/shard_map/all_to_all | solution.py:162
  1279.4 26.7 %reduce.1 = f32[8,262144]{1,0:T(8,128)} reduce(f32[8,1,262144]{2,1,0:T(1,128)} %all-to-all-done.5, f32[]{:T(128)} %broadcast.344), dimensions={1}, to_apply=%all_to_all.72.reduce_sub_computation | reduce | bytes 16777220 | tf_op jit(solution)/shard_map/all_to_all | solution.py:162
  1306.1 15.7 %reshape.656 = f32[4096,8,64]{2,1,0:T(8,128)} reshape(f32[8,262144]{1,0:T(8,128)} %reduce.1) | data formatting | bytes 16777216
  1321.8 12.8 copy.230
  1334.6 38.3 %fusion.12 = f32[64,64,512]{2,0,1:T(8,128)S(1)} fusion(f32[64,64,512]{2,0,1:T(8,128)} %fusion.27, f32[64,1,64,512]{3,2,1,0:T(8,128)} %get-tuple-element.9, f32[64,1,64,512]{3,2,1,0:T(8,128)} %get-tuple-element.8, f32[64,1,64,512]{3,2,1,0:T(8,128)} %get-tuple-element.6, f32[64,8,8,512]{3,0,1,2:T(8,128)} %copy.230, f32[64,4,4,4,512]{4,0,3,2,1:T(8,128)} %copy.226, ...), kind=kLoop, calls=%fused_computation.24 | loop fusion | flops 27262976 | bytes 67518464 | tf_op jit(solution)/shard_map/add | solution.py:174
  1372.9 8.3 copy.232
  (537 shorter events, 360.5 us)
Async XLA Ops:
  11.6 7.1 copy-start.12
  11.6 134.2 %copy-start.30 = (s32[1,4,48]{2,1,0:T(4,128)S(1)}, s32[1,4,48]{2,1,0:T(4,128)}, u32[]{:S(2)}) copy-start(s32[1,4,48]{2,1,0:T(4,128)} %param.20) | copy-start | bytes 2308
  11.6 191.0 %all-to-all-start.1 = ((f32[64,64,512]{2,0,1:T(8,128)}), f32[64,64,512]{2,0,1:T(8,128)}, u32[]{:S(2)}, u32[]{:S(2)}) async-start(f32[64,64,512]{2,0,1:T(8,128)} %copy.231), calls=%async_computation.1 | async-start | bytes 16777216 | tf_op jit(solution)/shard_map/all_to_all | solution.py:166
  146.0 4.6 copy-start.3
  151.6 4.6 copy-start.5
  186.3 14.5 %copy-start.28 = (s32[1024]{0:T(1024)}, s32[1024]{0:T(1024)S(1)}, u32[]{:S(2)}) copy-start(s32[1024]{0:T(1024)S(1)} %pad_clamp_fusion.1) | copy-start | bytes 12292
  202.6 181.9 %all-to-all-start = ((f32[4,48,16,512]{3,2,1,0:T(8,128)}), f32[4,48,16,512]{3,2,1,0:T(8,128)}, u32[]{:S(2)}, u32[]{:S(2)}) async-start(f32[4,48,16,512]{3,2,1,0:T(8,128)} %broadcast_select_fusion.3), calls=%async_computation | async-start | bytes 12582912 | tf_op jit(solution)/shard_map/all_to_all | solution.py:148
  208.1 30.2 %slice-start = ((s8[12582912]{0:T(1024)(128)(4,1)}), s8[4194304]{0:T(1024)(128)(4,1)S(1)}, s32[]{:S(2)}) async-start(s8[12582912]{0:T(1024)(128)(4,1)} %bitcast.1766), calls=%async_computation.6 | async-start | bytes 8388608
  208.1 30.2 %slice-start.1 = ((s8[12582912]{0:T(1024)(128)(4,1)}), s8[4194304]{0:T(1024)(128)(4,1)S(1)}, s32[]{:S(2)}) async-start(s8[12582912]{0:T(1024)(128)(4,1)} %bitcast.1766), calls=%async_computation.7 | async-start | bytes 8388608
  216.5 117.9 %copy-start = (f32[64,8,8,512]{3,2,1,0:T(8,128)}, f32[64,8,8,512]{3,2,1,0:T(8,128)S(1)}, u32[]{:S(2)}) copy-start(f32[64,8,8,512]{3,2,1,0:T(8,128)S(1)} %copy.207) | copy-start | bytes 25165828
  216.5 21.8 %slice-start.2 = ((s8[12582912]{0:T(1024)(128)(4,1)}), s8[4194304]{0:T(1024)(128)(4,1)S(1)}, s32[]{:S(2)}) async-start(s8[12582912]{0:T(1024)(128)(4,1)} %bitcast.1766), calls=%async_computation.8 | async-start | bytes 8388608
  384.4 5.4 copy-start.36
  384.4 5.4 copy-start.25
  384.4 5.5 copy-start.35
  384.4 6.0 copy-start.39
  384.5 6.3 copy-start.21
  384.5 189.2 %all-to-all-start.2 = ((f32[8,1,262144]{2,1,0:T(1,128)}), f32[8,1,262144]{2,1,0:T(1,128)}, u32[]{:S(2)}, u32[]{:S(2)}) async-start(f32[8,1,262144]{2,1,0:T(1,128)} %reshape.653), calls=%async_computation.2 | async-start | bytes 16777216 | tf_op jit(solution)/shard_map/all_to_all | solution.py:162
  390.0 238.9 %copy-start.19 = (f32[64,64]{0,1:T(8,128)}, f32[64,64]{0,1:T(8,128)S(1)}, u32[]{:S(2)}) copy-start(f32[64,64]{0,1:T(8,128)S(1)} %copy.205) | copy-start | bytes 49156
  390.3 43.9 %copy-start.23 = (f32[577]{0:T(1024)}, f32[577]{0:T(1024)S(1)}, u32[]{:S(2)}) copy-start(f32[577]{0:T(1024)S(1)} %pad.59.clone) | copy-start | bytes 6928
  390.7 96.9 %copy-start.10 = (f32[64,6,512]{2,0,1:T(8,128)}, f32[64,6,512]{2,0,1:T(8,128)S(1)}, u32[]{:S(2)}) copy-start(f32[64,6,512]{2,0,1:T(8,128)S(1)} %fusion.106) | copy-start | bytes 2359300
  390.7 59.6 %copy-start.26 = (s32[1024]{0:T(1024)}, s32[1024]{0:T(1024)S(1)}, u32[]{:S(2)}) copy-start(s32[1024]{0:T(1024)S(1)} %pad_clamp_fusion) | copy-start | bytes 12292
  390.7 71.9 %copy-start.31 = (pred[384]{0:T(512)(128)(4,1)}, pred[384]{0:T(512)(128)(4,1)S(1)}, u32[]{:S(2)}) copy-start(pred[384]{0:T(512)(128)(4,1)S(1)} %compare_and_fusion) | copy-start | bytes 1156
  390.8 238.1 %copy-start.13 = (f32[64,512]{1,0:T(8,128)}, f32[64,512]{1,0:T(8,128)S(1)}, u32[]{:S(2)}) copy-start(f32[64,512]{1,0:T(8,128)S(1)} %get-tuple-element.23) | copy-start | bytes 393220
  390.8 238.1 %copy-start.15 = (f32[64,512]{1,0:T(8,128)}, f32[64,512]{1,0:T(8,128)S(1)}, u32[]{:S(2)}) copy-start(f32[64,512]{1,0:T(8,128)S(1)} %get-tuple-element.24) | copy-start | bytes 393220
  390.8 238.1 %copy-start.17 = (f32[64,512]{1,0:T(8,128)}, f32[64,512]{1,0:T(8,128)S(1)}, u32[]{:S(2)}) copy-start(f32[64,512]{1,0:T(8,128)S(1)} %get-tuple-element.25) | copy-start | bytes 393220
  505.7 4.4 copy-start.9
  505.7 4.4 copy-start.37
  671.0 188.8 %all-to-all-start.4 = ((f32[64,64,512]{2,0,1:T(8,128)}), f32[64,64,512]{2,0,1:T(8,128)}, u32[]{:S(2)}, u32[]{:S(2)}) async-start(f32[64,64,512]{2,0,1:T(8,128)} %fusion.27), calls=%async_computation.4 | async-start | bytes 16777216 | tf_op jit(solution)/shard_map/all_to_all | solution.py:166
  676.0 4.6 copy-start.2
  681.6 4.6 copy-start.6
  701.4 14.7 %copy-start.29 = (s32[1024]{0:T(1024)S(1)}, s32[1024]{0:T(1024)}, u32[]{:S(2)}) copy-start(s32[1024]{0:T(1024)} %copy-done.28) | copy-start | bytes 12292
  716.1 8.2 copy-start.34
  859.9 230.6 %all-to-all-start.3 = ((f32[4,48,16,512]{3,2,1,0:T(8,128)}), f32[4,48,16,512]{3,2,1,0:T(8,128)}, u32[]{:S(2)}, u32[]{:S(2)}) async-start(f32[4,48,16,512]{3,2,1,0:T(8,128)} %broadcast_select_fusion.2), calls=%async_computation.3 | async-start | bytes 12582912 | tf_op jit(solution)/shard_map/all_to_all | solution.py:148
  873.3 8.5 copy-start.4
  881.9 122.2 %copy-start.1 = (f32[64,8,8,512]{3,1,2,0:T(8,128)}, f32[64,8,8,512]{3,1,2,0:T(8,128)S(1)}, u32[]{:S(2)}) copy-start(f32[64,8,8,512]{3,1,2,0:T(8,128)S(1)} %copy.256) | copy-start | bytes 25165828
  881.9 49.8 %slice-start.3 = ((s8[12582912]{0:T(1024)(128)(4,1)}), s8[4194304]{0:T(1024)(128)(4,1)S(1)}, s32[]{:S(2)}) async-start(s8[12582912]{0:T(1024)(128)(4,1)} %bitcast.1768), calls=%async_computation.9 | async-start | bytes 8388608
  901.1 30.6 %slice-start.4 = ((s8[12582912]{0:T(1024)(128)(4,1)}), s8[4194304]{0:T(1024)(128)(4,1)S(1)}, s32[]{:S(2)}) async-start(s8[12582912]{0:T(1024)(128)(4,1)} %bitcast.1768), calls=%async_computation.10 | async-start | bytes 8388608
  917.5 14.2 %slice-start.5 = ((s8[12582912]{0:T(1024)(128)(4,1)}), s8[4194304]{0:T(1024)(128)(4,1)S(1)}, s32[]{:S(2)}) async-start(s8[12582912]{0:T(1024)(128)(4,1)} %bitcast.1768), calls=%async_computation.11 | async-start | bytes 8388608
  1090.4 5.1 copy-start.22
  1090.4 189.0 %all-to-all-start.5 = ((f32[8,1,262144]{2,1,0:T(1,128)}), f32[8,1,262144]{2,1,0:T(1,128)}, u32[]{:S(2)}, u32[]{:S(2)}) async-start(f32[8,1,262144]{2,1,0:T(1,128)} %reshape.655), calls=%async_computation.5 | async-start | bytes 16777216 | tf_op jit(solution)/shard_map/all_to_all | solution.py:162
  1125.4 18.3 %copy-start.24 = (f32[577]{0:T(1024)S(1)}, f32[577]{0:T(1024)}, u32[]{:S(2)}) copy-start(f32[577]{0:T(1024)} %copy-done.23) | copy-start | bytes 6928
  1143.8 16.1 %copy-start.27 = (s32[1024]{0:T(1024)S(1)}, s32[1024]{0:T(1024)}, u32[]{:S(2)}) copy-start(s32[1024]{0:T(1024)} %copy-done.26) | copy-start | bytes 12292
  1159.9 12.3 copy-start.32
  1182.6 14.6 %copy-start.11 = (f32[64,6,512]{2,0,1:T(8,128)S(1)}, f32[64,6,512]{2,0,1:T(8,128)}, u32[]{:S(2)}) copy-start(f32[64,6,512]{2,0,1:T(8,128)} %copy-done.10) | copy-start | bytes 2359300
  1321.8 12.8 copy-start.14
  1321.8 12.8 copy-start.16
  1321.8 12.8 copy-start.18
  1321.8 12.8 copy-start.20
  (4 other events, 13.3 us)
where the time goes:
time: 1390 us; the launch traced here: 1380 us
  local copies, waits for them, and re-layouts  413 us (30%)
  matrix products  321 us (23%)
  other arithmetic  261 us (19%)
  waiting for transfers between devices  231 us (17%)
  between operations  123 us (9%)
  starting transfers between devices  33.1 us (2%)
    dot_general x384, matrix products, collide(): lax.dot_general(piece, collision_blocks[block_id, slot], (((1,), (1,)), (...  266 us
    all_to_all x2, waiting for transfers between devices, to_nodes(): lax.all_to_all(node_field, 'vel', split_axis=1, concat_axis=2, tiled=True)  131 us
    unnamed x114, local copies, waits for them, and re-layouts  107 us
    all_to_all x2, waiting for transfers between devices, on_nodes(): lax.all_to_all(change, 'vel', split_axis=2, concat_axis=1, tiled=True)  99.1 us
    dot_general x2, matrix products, advection(): jnp.einsum('mn,env->emv', stacked, node_field, precision=lax.Precision.HI...  55 us
    all_to_all x2, other arithmetic, on_nodes(): lax.all_to_all(change, 'vel', split_axis=2, concat_axis=1, tiled=True)  52.9 us
    add x1, other arithmetic, body(): first_section = distribution + TIME_STEP * (flow_zero + scaling * back_zero)  42.2 us
    add x1, other arithmetic, body(): 0.5 * distribution  38.3 us
  transfers between devices with their start and end apart: 6, of which 4 were waited for; matrix products, arithmetic and copies ran while one was open for 55% of the time, Pallas kernels for 0%

commit v1 on v0

--- a/solution.py
+++ b/solution.py
@@ -7,6 +7,13 @@
 VG = 16
 TIME_STEP = 0.03
 LIFT_SCALE = 6.0
+
+
+def exchange_blocks(x, axis, split, join):
+    count = lax.axis_size(axis)
+    pieces = jnp.stack(jnp.split(x, count, axis=split), axis=0)
+    pieces = lax.all_to_all(pieces, axis, split_axis=0, concat_axis=0)
+    return jnp.concatenate(pieces, axis=join)
 
 
 def lagrange_derivative():
@@ -159,7 +166,7 @@
 
     def on_nodes(node_block):
         change = collide(node_block, collision_blocks, block_columns)
-        returned = lax.all_to_all(change, "vel", split_axis=2, concat_axis=1, tiled=True)
+        returned = exchange_blocks(change, "vel", 2, 1)
         return (returned, node_block, change)
 
     def to_nodes(node_field):

time: 1390 us -> 1290 us (0.928)
  local copies, waits for them, and re-layouts: 413 us -> 352 us
  other arithmetic: 261 us -> 224 us
    all_to_all x2 -> x0, other arithmetic: 52.9 us -> none  [on_nodes(): lax.all_to_all(change, 'vel', split_axis=2, concat_axis=1, tiled=True)]
    unnamed x114 -> x126, local copies, waits for them, and re-layouts: 107 us -> 78.2 us
    sub x2 -> x0, local copies, waits for them, and re-layouts: 26.7 us -> none  [collide(): return applied - node_block]
    all_to_all x3 -> x0, local copies, waits for them, and re-layouts: 26 us -> none  [on_nodes(): lax.all_to_all(change, 'vel', split_axis=2, concat_axis=1, tiled=True)]
  transfers between devices with their start and end apart: 6 -> 6, of which waited for: 4 -> 4; matrix products, arithmetic and copies ran while one was open for 55% -> 58% of each run, Pallas kernels for 0% -> 0%
where the time goes in v1:
time: 1290 us; the launch traced here: 1270 us
  local copies, waits for them, and re-layouts  352 us (27%)
  matrix products  313 us (24%)
  waiting for transfers between devices  231 us (18%)
  other arithmetic  224 us (17%)
  between operations  123 us (10%)
  starting transfers between devices  33 us (3%)
    dot_general x384, matrix products, collide(): lax.dot_general(piece, collision_blocks[block_id, slot], (((1,), (1,)), (...  258 us
    all_to_all x2, waiting for transfers between devices, to_nodes(): lax.all_to_all(node_field, 'vel', split_axis=1, concat_axis=2, tiled=True)  132 us
    all_to_all x2, waiting for transfers between devices, exchange_blocks(): pieces = lax.all_to_all(pieces, axis, split_axis=0, concat_axis=0)  98.9 us
    unnamed x126, local copies, waits for them, and re-layouts  78.2 us
    dot_general x2, matrix products, advection(): jnp.einsum('mn,env->emv', stacked, node_field, precision=lax.Precision.HI...  55 us
    add x1, other arithmetic, body(): first_section = distribution + TIME_STEP * (flow_zero + scaling * back_zero)  52.3 us
    add x1, other arithmetic, body(): 0.5 * distribution  44.3 us
    slice x2, local copies, waits for them, and re-layouts, advection(): derived[:, 0]  36.6 us
  transfers between devices with their start and end apart: 6, of which 4 were waited for; matrix products, arithmetic and copies ran while one was open for 58% of the time, Pallas kernels for 0%

profile of v1, /device:TPU:0, one launch (start us, length us, event | category | flops | bytes accessed | tf_op | source)
XLA Modules:
  0.0 1274.8 jit_solution(3578454796269188615)
XLA Ops:
  0.0 11.6 copy.192
  11.6 7.1 all-to-all-start.1
  155.9 15.2 %copy.159 = f32[64,6,4,4,512]{4,3,2,1,0:T(4,128)} copy(f32[64,6,4,4,512]{4,0,3,2,1:T(8,128)S(1)} %fusion.37) | data formatting | bytes 25165824 | tf_op jit(solution)/shard_map/stack | solution.py:79
  171.1 14.7 %reshape_reshape.6 = f32[384,16,512]{2,1,0:T(8,128)} reshape(f32[64,6,4,4,512]{4,3,2,1,0:T(4,128)} %copy.159) | data formatting | bytes 25165824 | tf_op jit(solution)/shard_map/reshape;reshape | solution.py:153
  186.0 8.2 gather_fusion
  194.6 5.9 broadcast_select_fusion.3
  202.6 5.4 all-to-all-start
  208.1 8.4 copy.168
  335.6 8.9 copy.169
  344.5 11.3 bitcast_subtract_fusion.1
  374.1 5.1 all-to-all-start.2
  380.2 25.1 %fusion.1761 = f32[192,64,512]{2,0,1:T(8,128)} fusion(f32[192,64,1]{0,1,2:T(8,128)S(1)} %copy-done.22, f32[64,64,512]{2,1,0:T(8,128)} %param.15), kind=kOutput, calls=%fused_computation.2174 | convolution fusion | flops 4831838208 | bytes 33603584 | tf_op jit(solution)/shard_map/mn,env->emv/dot_general | solution.py:98
  405.3 18.3 %fusion.1747 = (f32[64,1,64,512]{3,2,1,0:T(8,128)}, f32[64,1,64,512]{3,2,1,0:T(8,128)}, f32[64,1,64,512]{3,2,1,0:T(8,128)}) fusion(f32[64,3,64,512]{3,2,1,0:T(8,128)} %bitcast.1808), kind=kLoop, calls=%fused_computation.2160 | loop fusion | bytes 50331648 | tf_op jit(solution)/shard_map/slice | solution.py:101
  423.6 16.1 %maximum_maximum_fusion = f32[577,16,512]{2,1,0:T(8,128)} fusion(f32[192,16,512]{2,1,0:T(8,128)} %bitcast.18, f32[384,16,512]{2,1,0:T(8,128)} %reshape_reshape.6, f32[577]{0:T(1024)S(1)} %pad.59.clone), kind=kLoop, calls=%fused_computation.4 | loop fusion | flops 9453568 | bytes 37783812 | tf_op jit(solution)/shard_map/concatenate | solution.py:156
  439.7 12.3 gather_fusion.1
  452.0 10.5 broadcast_select_fusion.1
  462.5 14.5 %reshape.602 = f32[64,6,4,4,512]{4,3,2,1,0:T(4,128)} reshape(f32[384,16,512]{2,1,0:T(8,128)} %broadcast_select_fusion.1) | data formatting | bytes 25165824 | tf_op jit(solution)/shard_map/reshape | solution.py:164
  477.0 13.8 %fusion.1 = f32[64,6,4,4,512]{4,0,3,2,1:T(8,128)S(1)} fusion(f32[64,6,4,4,512]{4,0,3,2,1:T(8,128)} %copy-done.5, f32[64,6,4,4,512]{4,3,2,1,0:T(4,128)} %reshape.602, f32[64,6,512]{2,0,1:T(8,128)S(1)} %fusion.122), kind=kLoop, calls=%fused_computation.9 | loop fusion | flops 6291456 | bytes 38535168 | tf_op jit(solution)/shard_map/mul | solution.py:108
  503.9 8.5 copy.165
  512.5 50.6 %all-to-all-done.2 = f32[8,64,8,512]{3,2,1,0:T(8,128)} async-done(((f32[8,64,8,512]{3,2,1,0:T(8,128)}), f32[8,64,8,512]{3,2,1,0:T(8,128)}, u32[]{:S(2)}, u32[]{:S(2)}) %all-to-all-start.2) | async-done | bytes 8388640 | tf_op jit(solution)/shard_map/all_to_all | solution.py:15
  563.1 8.1 copy_bitcast_fusion.8
  571.2 52.3 %fusion.27 = f32[64,64,512]{2,0,1:T(8,128)} fusion(f32[64,1,64,512]{3,2,1,0:T(8,128)} %get-tuple-element.12, f32[64,1,64,512]{3,2,1,0:T(8,128)} %get-tuple-element.11, f32[64,1,64,512]{3,2,1,0:T(8,128)} %get-tuple-element.10, f32[64,4,4,4,512]{4,0,3,2,1:T(8,128)} %copy.165, f32[64,64,512]{2,1,0:T(8,128)} %copy_bitcast_fusion.8, f32[64,64]{0,1:T(8,128)S(1)} %copy.166, ...), kind=kLoop, calls=%fused_computation.43 | loop fusion | flops 23068672 | bytes 59129856 | tf_op jit(solution)/shard_map/add | solution.py:178
  623.5 4.9 all-to-all-start.4
  638.7 15.2 %copy.181 = f32[64,6,4,4,512]{4,3,2,1,0:T(4,128)} copy(f32[64,6,4,4,512]{4,0,3,2,1:T(8,128)S(1)} %fusion.33) | data formatting | bytes 25165824 | tf_op jit(solution)/shard_map/stack | solution.py:79
  653.9 14.7 %reshape_reshape.7 = f32[384,16,512]{2,1,0:T(8,128)} reshape(f32[64,6,4,4,512]{4,3,2,1,0:T(4,128)} %copy.181) | data formatting | bytes 25165824 | tf_op jit(solution)/shard_map/reshape;reshape | solution.py:153
  668.5 8.2 gather_fusion.2
  676.8 5.9 broadcast_select_fusion.2
  682.7 129.6 %all-to-all-done.4 = f32[64,64,512]{2,0,1:T(8,128)} async-done(((f32[64,64,512]{2,0,1:T(8,128)}), f32[64,64,512]{2,0,1:T(8,128)}, u32[]{:S(2)}, u32[]{:S(2)}) %all-to-all-start.4) | async-done | bytes 8388640 | tf_op jit(solution)/shard_map/all_to_all | solution.py:173
  812.3 5.4 all-to-all-start.3
  817.7 8.2 copy.322
  826.0 8.5 copy.217
  967.8 9.4 all_to_all.48
  985.3 9.1 copy.189
  994.4 11.2 bitcast_subtract_fusion
  1024.0 5.1 all-to-all-start.5
  1029.0 29.9 %fusion.31 = f32[64,512,192]{1,2,0:T(8,128)} fusion(f32[192,64,1]{0,1,2:T(8,128)S(1)} %copy-done.23, f32[64,64,512]{2,0,1:T(8,128)} %fusion.27), kind=kOutput, calls=%fused_computation.55 | convolution fusion | flops 4831838208 | bytes 33603584 | tf_op jit(solution)/shard_map/mn,env->emv/dot_general | solution.py:98
  1058.9 18.3 %fusion.1746 = (f32[64,1,64,512]{3,2,1,0:T(8,128)}, f32[64,1,64,512]{3,2,1,0:T(8,128)}, f32[64,1,64,512]{3,2,1,0:T(8,128)}) fusion(f32[64,3,64,512]{3,2,1,0:T(8,128)} %bitcast.1809), kind=kLoop, calls=%fused_computation.2159 | loop fusion | bytes 50331648 | tf_op jit(solution)/shard_map/slice | solution.py:101
  1077.2 16.1 %maximum_maximum_fusion.1 = f32[577,16,512]{2,1,0:T(8,128)} fusion(f32[192,16,512]{2,1,0:T(8,128)} %bitcast.436, f32[384,16,512]{2,1,0:T(8,128)} %reshape_reshape.7, f32[577]{0:T(1024)S(1)} %copy-done.25), kind=kLoop, calls=%fused_computation.5 | loop fusion | flops 9453568 | bytes 37783812 | tf_op jit(solution)/shard_map/concatenate | solution.py:156
  1093.3 12.3 gather_fusion.3
  1105.7 10.5 broadcast_select_fusion
  1116.1 14.6 %reshape.611 = f32[64,6,4,4,512]{4,3,2,1,0:T(4,128)} reshape(f32[384,16,512]{2,1,0:T(8,128)} %broadcast_select_fusion) | data formatting | bytes 25165824 | tf_op jit(solution)/shard_map/reshape | solution.py:164
  1130.7 13.8 %fusion = f32[64,6,4,4,512]{4,0,3,2,1:T(8,128)S(1)} fusion(f32[64,6,4,4,512]{4,0,3,2,1:T(8,128)} %copy-done.6, f32[64,6,4,4,512]{4,3,2,1,0:T(4,128)} %reshape.611, f32[64,6,512]{2,0,1:T(8,128)S(1)} %copy-done.12), kind=kLoop, calls=%fused_computation.7 | loop fusion | flops 6291456 | bytes 38535168 | tf_op jit(solution)/shard_map/mul | solution.py:108
  1148.8 7.3 fusion.3
  1156.1 8.5 copy.187
  1164.6 48.3 %all-to-all-done.5 = f32[8,64,8,512]{3,2,1,0:T(8,128)} async-done(((f32[8,64,8,512]{3,2,1,0:T(8,128)}), f32[8,64,8,512]{3,2,1,0:T(8,128)}, u32[]{:S(2)}, u32[]{:S(2)}) %all-to-all-start.5) | async-done | bytes 8388640 | tf_op jit(solution)/shard_map/all_to_all | solution.py:15
  1212.9 4.6 copy_bitcast_fusion.6
  1218.7 44.3 %fusion.12 = f32[64,64,512]{2,0,1:T(8,128)} fusion(f32[64,64,512]{2,0,1:T(8,128)} %fusion.27, f32[64,1,64,512]{3,2,1,0:T(8,128)} %get-tuple-element.9, f32[64,1,64,512]{3,2,1,0:T(8,128)} %get-tuple-element.8, f32[64,1,64,512]{3,2,1,0:T(8,128)} %get-tuple-element.6, f32[64,4,4,4,512]{4,0,3,2,1:T(8,128)S(1)} %copy-done.7, ...), kind=kLoop, calls=%fused_computation.24 | loop fusion | flops 27262976 | bytes 67518464 | tf_op jit(solution)/shard_map/add | solution.py:181
  1262.9 11.6 copy.193
  (546 shorter events, 344.4 us)
Async XLA Ops:
  11.6 7.1 copy-start.13
  11.6 134.0 %copy-start.31 = (s32[1,4,48]{2,1,0:T(4,128)S(1)}, s32[1,4,48]{2,1,0:T(4,128)}, u32[]{:S(2)}) copy-start(s32[1,4,48]{2,1,0:T(4,128)} %param.20) | copy-start | bytes 2308
  11.6 191.0 %all-to-all-start.1 = ((f32[64,64,512]{2,0,1:T(8,128)}), f32[64,64,512]{2,0,1:T(8,128)}, u32[]{:S(2)}, u32[]{:S(2)}) async-start(f32[64,64,512]{2,0,1:T(8,128)} %copy.192), calls=%async_computation.1 | async-start | bytes 16777216 | tf_op jit(solution)/shard_map/all_to_all | solution.py:173
  145.7 4.6 copy-start.3
  151.3 4.6 copy-start.5
  185.9 14.6 %copy-start.29 = (s32[1024]{0:T(1024)}, s32[1024]{0:T(1024)S(1)}, u32[]{:S(2)}) copy-start(s32[1024]{0:T(1024)S(1)} %pad_clamp_fusion.1) | copy-start | bytes 12292
  202.6 171.5 %all-to-all-start = ((f32[4,48,16,512]{3,2,1,0:T(8,128)}), f32[4,48,16,512]{3,2,1,0:T(8,128)}, u32[]{:S(2)}, u32[]{:S(2)}) async-start(f32[4,48,16,512]{3,2,1,0:T(8,128)} %broadcast_select_fusion.3), calls=%async_computation | async-start | bytes 12582912 | tf_op jit(solution)/shard_map/all_to_all | solution.py:155
  208.0 30.2 %slice-start = ((s8[12582912]{0:T(1024)(128)(4,1)}), s8[4194304]{0:T(1024)(128)(4,1)S(1)}, s32[]{:S(2)}) async-start(s8[12582912]{0:T(1024)(128)(4,1)} %bitcast.1818), calls=%async_computation.6 | async-start | bytes 8388608
  208.1 30.2 %slice-start.1 = ((s8[12582912]{0:T(1024)(128)(4,1)}), s8[4194304]{0:T(1024)(128)(4,1)S(1)}, s32[]{:S(2)}) async-start(s8[12582912]{0:T(1024)(128)(4,1)} %bitcast.1818), calls=%async_computation.7 | async-start | bytes 8388608
  216.5 118.0 %copy-start = (f32[64,8,8,512]{3,2,1,0:T(8,128)}, f32[64,8,8,512]{3,2,1,0:T(8,128)S(1)}, u32[]{:S(2)}) copy-start(f32[64,8,8,512]{3,2,1,0:T(8,128)S(1)} %copy.168) | copy-start | bytes 25165828
  216.5 21.8 %slice-start.2 = ((s8[12582912]{0:T(1024)(128)(4,1)}), s8[4194304]{0:T(1024)(128)(4,1)S(1)}, s32[]{:S(2)}) async-start(s8[12582912]{0:T(1024)(128)(4,1)} %bitcast.1818), calls=%async_computation.8 | async-start | bytes 8388608
  374.1 5.1 copy-start.37
  374.1 5.2 copy-start.26
  374.1 5.3 copy-start.36
  374.1 5.8 copy-start.40
  374.1 6.1 copy-start.22
  374.1 189.0 %all-to-all-start.2 = ((f32[8,64,8,512]{3,2,1,0:T(8,128)}), f32[8,64,8,512]{3,2,1,0:T(8,128)}, u32[]{:S(2)}, u32[]{:S(2)}) async-start(f32[8,64,8,512]{3,2,1,0:T(8,128)} %fusion.113), calls=%async_computation.2 | async-start | bytes 16777216 | tf_op jit(solution)/shard_map/all_to_all | solution.py:15
  379.3 191.9 %copy-start.20 = (f32[64,64]{0,1:T(8,128)}, f32[64,64]{0,1:T(8,128)S(1)}, u32[]{:S(2)}) copy-start(f32[64,64]{0,1:T(8,128)S(1)} %copy.166) | copy-start | bytes 49156
  379.7 44.0 %copy-start.24 = (f32[577]{0:T(1024)}, f32[577]{0:T(1024)S(1)}, u32[]{:S(2)}) copy-start(f32[577]{0:T(1024)S(1)} %pad.59.clone) | copy-start | bytes 6928
  380.1 96.9 %copy-start.11 = (f32[64,6,512]{2,0,1:T(8,128)}, f32[64,6,512]{2,0,1:T(8,128)S(1)}, u32[]{:S(2)}) copy-start(f32[64,6,512]{2,0,1:T(8,128)S(1)} %fusion.122) | copy-start | bytes 2359300
  380.1 59.6 %copy-start.27 = (s32[1024]{0:T(1024)}, s32[1024]{0:T(1024)S(1)}, u32[]{:S(2)}) copy-start(s32[1024]{0:T(1024)S(1)} %pad_clamp_fusion) | copy-start | bytes 12292
  380.1 71.9 %copy-start.32 = (pred[384]{0:T(512)(128)(4,1)}, pred[384]{0:T(512)(128)(4,1)S(1)}, u32[]{:S(2)}) copy-start(pred[384]{0:T(512)(128)(4,1)S(1)} %compare_and_fusion) | copy-start | bytes 1156
  380.2 191.0 %copy-start.14 = (f32[64,512]{1,0:T(8,128)}, f32[64,512]{1,0:T(8,128)S(1)}, u32[]{:S(2)}) copy-start(f32[64,512]{1,0:T(8,128)S(1)} %get-tuple-element.23) | copy-start | bytes 393220
  380.2 191.0 %copy-start.16 = (f32[64,512]{1,0:T(8,128)}, f32[64,512]{1,0:T(8,128)S(1)}, u32[]{:S(2)}) copy-start(f32[64,512]{1,0:T(8,128)S(1)} %get-tuple-element.24) | copy-start | bytes 393220
  380.2 191.0 %copy-start.18 = (f32[64,512]{1,0:T(8,128)}, f32[64,512]{1,0:T(8,128)S(1)}, u32[]{:S(2)}) copy-start(f32[64,512]{1,0:T(8,128)S(1)} %get-tuple-element.25) | copy-start | bytes 393220
  495.0 4.4 copy-start.38
  623.5 188.8 %all-to-all-start.4 = ((f32[64,64,512]{2,0,1:T(8,128)}), f32[64,64,512]{2,0,1:T(8,128)}, u32[]{:S(2)}, u32[]{:S(2)}) async-start(f32[64,64,512]{2,0,1:T(8,128)} %fusion.27), calls=%async_computation.4 | async-start | bytes 16777216 | tf_op jit(solution)/shard_map/all_to_all | solution.py:173
  628.5 4.6 copy-start.2
  634.1 4.6 copy-start.6
  653.9 14.7 %copy-start.30 = (s32[1024]{0:T(1024)S(1)}, s32[1024]{0:T(1024)}, u32[]{:S(2)}) copy-start(s32[1024]{0:T(1024)} %copy-done.29) | copy-start | bytes 12292
  668.5 8.2 copy-start.35
  812.3 211.6 %all-to-all-start.3 = ((f32[4,48,16,512]{3,2,1,0:T(8,128)}), f32[4,48,16,512]{3,2,1,0:T(8,128)}, u32[]{:S(2)}, u32[]{:S(2)}) async-start(f32[4,48,16,512]{3,2,1,0:T(8,128)} %broadcast_select_fusion.2), calls=%async_computation.3 | async-start | bytes 12582912 | tf_op jit(solution)/shard_map/all_to_all | solution.py:155
  826.0 8.5 copy-start.4
  834.5 132.1 %copy-start.1 = (f32[64,8,8,512]{3,1,2,0:T(8,128)}, f32[64,8,8,512]{3,1,2,0:T(8,128)S(1)}, u32[]{:S(2)}) copy-start(f32[64,8,8,512]{3,1,2,0:T(8,128)S(1)} %copy.217) | copy-start | bytes 25165828
  834.5 50.0 %slice-start.3 = ((s8[12582912]{0:T(1024)(128)(4,1)}), s8[4194304]{0:T(1024)(128)(4,1)S(1)}, s32[]{:S(2)}) async-start(s8[12582912]{0:T(1024)(128)(4,1)} %bitcast.1820), calls=%async_computation.9 | async-start | bytes 8388608
  853.8 30.7 %slice-start.4 = ((s8[12582912]{0:T(1024)(128)(4,1)}), s8[4194304]{0:T(1024)(128)(4,1)S(1)}, s32[]{:S(2)}) async-start(s8[12582912]{0:T(1024)(128)(4,1)} %bitcast.1820), calls=%async_computation.10 | async-start | bytes 8388608
  870.2 14.3 %slice-start.5 = ((s8[12582912]{0:T(1024)(128)(4,1)}), s8[4194304]{0:T(1024)(128)(4,1)S(1)}, s32[]{:S(2)}) async-start(s8[12582912]{0:T(1024)(128)(4,1)} %bitcast.1820), calls=%async_computation.11 | async-start | bytes 8388608
  1024.0 5.1 copy-start.23
  1024.0 188.9 %all-to-all-start.5 = ((f32[8,64,8,512]{3,2,1,0:T(8,128)}), f32[8,64,8,512]{3,2,1,0:T(8,128)}, u32[]{:S(2)}, u32[]{:S(2)}) async-start(f32[8,64,8,512]{3,2,1,0:T(8,128)} %fusion.105), calls=%async_computation.5 | async-start | bytes 16777216 | tf_op jit(solution)/shard_map/all_to_all | solution.py:15
  1058.9 18.3 %copy-start.25 = (f32[577]{0:T(1024)S(1)}, f32[577]{0:T(1024)}, u32[]{:S(2)}) copy-start(f32[577]{0:T(1024)} %copy-done.24) | copy-start | bytes 6928
  1077.2 16.1 %copy-start.28 = (s32[1024]{0:T(1024)S(1)}, s32[1024]{0:T(1024)}, u32[]{:S(2)}) copy-start(s32[1024]{0:T(1024)} %copy-done.27) | copy-start | bytes 12292
  1093.3 12.3 copy-start.33
  1116.1 14.6 %copy-start.12 = (f32[64,6,512]{2,0,1:T(8,128)S(1)}, f32[64,6,512]{2,0,1:T(8,128)}, u32[]{:S(2)}) copy-start(f32[64,6,512]{2,0,1:T(8,128)} %copy-done.11) | copy-start | bytes 2359300
  1164.6 52.9 %copy-start.15 = (f32[64,512]{1,0:T(8,128)S(1)}, f32[64,512]{1,0:T(8,128)}, u32[]{:S(2)}) copy-start(f32[64,512]{1,0:T(8,128)} %copy-done.14) | copy-start | bytes 393220
  1164.6 52.9 %copy-start.17 = (f32[64,512]{1,0:T(8,128)S(1)}, f32[64,512]{1,0:T(8,128)}, u32[]{:S(2)}) copy-start(f32[64,512]{1,0:T(8,128)} %copy-done.16) | copy-start | bytes 393220
  1164.6 52.9 %copy-start.19 = (f32[64,512]{1,0:T(8,128)S(1)}, f32[64,512]{1,0:T(8,128)}, u32[]{:S(2)}) copy-start(f32[64,512]{1,0:T(8,128)} %copy-done.18) | copy-start | bytes 393220
  1164.6 53.0 %copy-start.21 = (f32[64,64]{0,1:T(8,128)S(1)}, f32[64,64]{0,1:T(8,128)}, u32[]{:S(2)}) copy-start(f32[64,64]{0,1:T(8,128)} %copy-done.20) | copy-start | bytes 49156
  1212.9 5.8 copy-start.7
  (5 other events, 17.8 us)
